TPU v7x, 32 devices: a whole 2x2x4 slice. The times are simulated.
32 devices in a mesh: gx: 4 (over x, core), gy: 8 (over z, y).
Axes of the slice: x: 2, y: 2, z: 4, core: 2. Of those that a mesh axis runs over, the one named last changes fastest.
Arguments:
- layer_input: bfloat16 [8192, 1152], P(('gx', 'gy')), may hold values from -6 to 6
- norm_one_gain: bfloat16 [1152], P('gy'), may hold values from 0.5 to 1.5
- norm_one_bias: bfloat16 [1152], P('gy'), may hold values from -1.75 to 1.75
- query_weight: bfloat16 [1152, 1152], P('gx', 'gy'), may hold values from -0.1875 to 0.1875
- query_bias: bfloat16 [1152], P('gy'), may hold values from -1.75 to 1.75
- key_weight: bfloat16 [1152, 1152], P('gx', 'gy'), may hold values from -0.1875 to 0.1875
- value_weight: bfloat16 [1152, 1152], P('gx', 'gy'), may hold values from -0.1875 to 0.1875
- value_bias: bfloat16 [1152], P('gy'), may hold values from -1.75 to 1.75
- output_weight: bfloat16 [1152, 1152], P('gy', 'gx'), may hold values from -1 to 1
- output_bias: bfloat16 [1152], P('gy'), may hold values from -1.75 to 1.75
- norm_two_gain: bfloat16 [1152], P('gy'), may hold values from 0.5 to 1.5
- norm_two_bias: bfloat16 [1152], P('gy'), may hold values from -1.75 to 1.75
- up_weight: bfloat16 [1152, 4304], P('gx', 'gy'), may hold values from -0.1875 to 0.1875
- up_bias: bfloat16 [4304], P('gy'), may hold values from -1.75 to 1.75
- down_weight: bfloat16 [4304, 1152], P('gy', 'gx'), may hold values from -0.09375 to 0.09375
- down_bias: bfloat16 [1152], P('gy'), may hold values from -1.75 to 1.75
- cotangent: bfloat16 [8192, 1152], P(('gx', 'gy')), may hold values from -6 to 6
Outputs:
- layer_output: bfloat16 [8192, 1152], P(('gx', 'gy'))
- grad_input: bfloat16 [8192, 1152], P(('gx', 'gy'))
- grad_norm_one_gain: float32 [1152], P('gy')
- grad_norm_one_bias: float32 [1152], P('gy')
- grad_query_weight: float32 [1152, 1152], P('gx', 'gy')
- grad_query_bias: float32 [1152], P('gy')
- grad_key_weight: float32 [1152, 1152], P('gx', 'gy')
- grad_value_weight: float32 [1152, 1152], P('gx', 'gy')
- grad_value_bias: float32 [1152], P('gy')
- grad_output_weight: float32 [1152, 1152], P('gy', 'gx')
- grad_output_bias: float32 [1152], P('gy')
- grad_norm_two_gain: float32 [1152], P('gy')
- grad_norm_two_bias: float32 [1152], P('gy')
- grad_up_weight: float32 [1152, 4304], P('gx', 'gy')
- grad_up_bias: float32 [4304], P('gy')
- grad_down_weight: float32 [4304, 1152], P('gy', 'gx')
- grad_down_bias: float32 [1152], P('gy')
All inputs are finite; a program needn't handle non-finite values.
Results may differ from a plain program's by a relative error of at most 0.023.
Values may be sent and summed in bfloat16 or wider, within the bound.
A program may use at most 192 MiB of HBM per device.

v0:
```python
import jax
import jax.numpy as jnp
from jax import lax
from jax.sharding import PartitionSpec as P

HD = 72
LENGTH = 1024


def dot_plain(left, right):
    return jnp.dot(left, right, preferred_element_type=jnp.float32)


def dot_right_t(left, right):
    return lax.dot_general(
        left, right, (((1,), (1,)), ((), ())), preferred_element_type=jnp.float32
    )


def dot_left_t(left, right):
    return lax.dot_general(
        left, right, (((0,), (0,)), ((), ())), preferred_element_type=jnp.float32
    )


def normalize(rows):
    center = rows - jnp.mean(rows, axis=-1, keepdims=True)
    inverse = lax.rsqrt(jnp.mean(center * center, axis=-1, keepdims=True) + 1e-06)
    return (center * inverse, inverse)


def gelu_tanh(value):
    return jax.nn.gelu(value, approximate=True)


def image_shape(array):
    heads = array.shape[1] // HD
    return (array.shape[0] // LENGTH, LENGTH, heads, HD)


def attend(query, key, value):
    shape = image_shape(query)
    scale = HD ** (-0.5)

    def one_image(carry, pieces):
        q_img, k_img, v_img = pieces
        scores = (
            jnp.einsum("qhd,khd->hqk", q_img, k_img, preferred_element_type=jnp.float32) * scale
        )
        top = jnp.max(scores, axis=-1, keepdims=True)
        expo = jnp.exp(scores - top)
        total = jnp.sum(expo, axis=-1, keepdims=True)
        probs = (expo / total).astype(jnp.bfloat16)
        mixed = jnp.einsum("hqk,khd->qhd", probs, v_img, preferred_element_type=jnp.float32).astype(
            jnp.bfloat16
        )
        return (carry, (mixed, (top + jnp.log(total))[..., 0]))

    _, (mixed, lse) = lax.scan(
        one_image, 0, (query.reshape(shape), key.reshape(shape), value.reshape(shape))
    )
    return (mixed.reshape(query.shape), lse)


def attend_back(query, key, value, lse, d_mixed):
    shape = image_shape(query)
    scale = HD ** (-0.5)

    def one_image(carry, pieces):
        q_img, k_img, v_img, lse_img, dm_img = pieces
        scores = (
            jnp.einsum("qhd,khd->hqk", q_img, k_img, preferred_element_type=jnp.float32) * scale
        )
        probs = jnp.exp(scores - lse_img[..., None])
        d_probs = jnp.einsum("qhd,khd->hqk", dm_img, v_img, preferred_element_type=jnp.float32)
        d_scores = (probs * (d_probs - jnp.sum(d_probs * probs, axis=-1, keepdims=True))).astype(
            jnp.bfloat16
        )
        d_value = jnp.einsum(
            "hqk,qhd->khd", probs.astype(jnp.bfloat16), dm_img, preferred_element_type=jnp.float32
        ).astype(jnp.bfloat16)
        d_query = (
            jnp.einsum("hqk,khd->qhd", d_scores, k_img, preferred_element_type=jnp.float32) * scale
        ).astype(jnp.bfloat16)
        d_key = (
            jnp.einsum("hqk,qhd->khd", d_scores, q_img, preferred_element_type=jnp.float32) * scale
        ).astype(jnp.bfloat16)
        return (carry, (d_query, d_key, d_value))

    _, (d_query, d_key, d_value) = lax.scan(
        one_image,
        0,
        (
            query.reshape(shape),
            key.reshape(shape),
            value.reshape(shape),
            lse,
            d_mixed.reshape(shape),
        ),
    )
    return (d_query.reshape(query.shape), d_key.reshape(query.shape), d_value.reshape(query.shape))


def forward_pass(
    complete,
    layer_input,
    norm_one_gain,
    norm_one_bias,
    query_weight,
    query_bias,
    key_weight,
    value_weight,
    value_bias,
    output_weight,
    output_bias,
    norm_two_gain,
    norm_two_bias,
    up_weight,
    up_bias,
    down_weight,
    down_bias,
):
    w_query, w_key, w_value, w_output, w_up, w_down = (
        lax.all_gather(query_weight, "gx", axis=0, tiled=True),
        lax.all_gather(key_weight, "gx", axis=0, tiled=True),
        lax.all_gather(value_weight, "gx", axis=0, tiled=True),
        lax.all_gather(output_weight, "gx", axis=1, tiled=True),
        lax.all_gather(up_weight, "gx", axis=0, tiled=True),
        lax.all_gather(down_weight, "gx", axis=1, tiled=True),
    )
    rows_one, gain_one, shift_one, out_shift, down_shift = (
        lax.all_gather(layer_input, "gy", axis=0, tiled=True),
        lax.all_gather(norm_one_gain, "gy", axis=0, tiled=True),
        lax.all_gather(norm_one_bias, "gy", axis=0, tiled=True),
        lax.all_gather(output_bias, "gy", axis=0, tiled=True),
        lax.all_gather(down_bias, "gy", axis=0, tiled=True),
    )
    hat_one, inv_one = normalize(rows_one.astype(jnp.float32))
    normed = (hat_one * gain_one.astype(jnp.float32) + shift_one.astype(jnp.float32)).astype(
        jnp.bfloat16
    )
    query = (dot_plain(normed, w_query) + query_bias.astype(jnp.float32)).astype(jnp.bfloat16)
    key = dot_plain(normed, w_key).astype(jnp.bfloat16)
    value = (dot_plain(normed, w_value) + value_bias.astype(jnp.float32)).astype(jnp.bfloat16)
    mixed, lse = attend(query, key, value)
    attn_part = lax.psum_scatter(
        dot_plain(mixed, w_output).astype(jnp.bfloat16), "gy", scatter_dimension=0, tiled=True
    ).astype(jnp.float32)
    residual = layer_input.astype(jnp.float32) + attn_part + out_shift.astype(jnp.float32)
    rows_two, gain_two, shift_two = (
        lax.all_gather(residual.astype(jnp.bfloat16), "gy", axis=0, tiled=True),
        lax.all_gather(norm_two_gain, "gy", axis=0, tiled=True),
        lax.all_gather(norm_two_bias, "gy", axis=0, tiled=True),
    )
    hat_two, inv_two = normalize(rows_two.astype(jnp.float32))
    normed_two = (hat_two * gain_two.astype(jnp.float32) + shift_two.astype(jnp.float32)).astype(
        jnp.bfloat16
    )
    upper = dot_plain(normed_two, w_up) + up_bias.astype(jnp.float32)
    active = gelu_tanh(upper).astype(jnp.bfloat16)
    result = residual
    if complete:
        mlp_part = lax.psum_scatter(
            dot_plain(active, w_down).astype(jnp.bfloat16), "gy", scatter_dimension=0, tiled=True
        ).astype(jnp.float32)
        result = residual + mlp_part + down_shift.astype(jnp.float32)
    return (
        w_query,
        w_key,
        w_value,
        w_output,
        w_up,
        w_down,
        hat_one,
        inv_one,
        normed,
        query,
        key,
        value,
        mixed,
        lse,
        hat_two,
        inv_two,
        normed_two,
        upper,
        active,
        result,
        gain_one,
        gain_two,
    )


def shards(
    layer_input,
    norm_one_gain,
    norm_one_bias,
    query_weight,
    query_bias,
    key_weight,
    value_weight,
    value_bias,
    output_weight,
    output_bias,
    norm_two_gain,
    norm_two_bias,
    up_weight,
    up_bias,
    down_weight,
    down_bias,
    cotangent,
):
    inputs = (
        layer_input,
        norm_one_gain,
        norm_one_bias,
        query_weight,
        query_bias,
        key_weight,
        value_weight,
        value_bias,
        output_weight,
        output_bias,
        norm_two_gain,
        norm_two_bias,
        up_weight,
        up_bias,
        down_weight,
        down_bias,
    )
    saved = forward_pass(True, *inputs)
    layer_output = saved[19].astype(jnp.bfloat16)
    again, layer_output = lax.optimization_barrier((inputs, layer_output))
    saved = forward_pass(False, *again)
    (
        w_query,
        w_key,
        w_value,
        w_output,
        w_up,
        w_down,
        hat_one,
        inv_one,
        normed,
        query,
        key,
        value,
        mixed,
        lse,
        hat_two,
        inv_two,
        normed_two,
        upper,
        active,
        result,
        gain_one,
        gain_two,
    ) = saved
    local = layer_input.shape[0]
    start = lax.axis_index("gy") * local
    grad_rows = lax.all_gather(cotangent, "gy", axis=0, tiled=True)
    d_active = dot_right_t(grad_rows, w_down)
    _, gelu_pull = jax.vjp(gelu_tanh, upper)
    d_upper = gelu_pull(d_active)[0].astype(jnp.bfloat16)
    grad_up_weight, grad_down_weight = (
        lax.psum_scatter(
            dot_left_t(normed_two, d_upper).astype(jnp.bfloat16),
            "gx",
            scatter_dimension=0,
            tiled=True,
        ).astype(jnp.float32),
        lax.psum_scatter(
            dot_left_t(active, grad_rows).astype(jnp.bfloat16),
            "gx",
            scatter_dimension=1,
            tiled=True,
        ).astype(jnp.float32),
    )
    d_normed_two = lax.psum_scatter(
        dot_right_t(d_upper, w_up).astype(jnp.bfloat16), "gy", scatter_dimension=0, tiled=True
    ).astype(jnp.float32)
    hat_two_local = lax.dynamic_slice_in_dim(hat_two, start, local, 0)
    inv_two_local = lax.dynamic_slice_in_dim(inv_two, start, local, 0)
    scaled_two = d_normed_two * gain_two.astype(jnp.float32)
    mean_two = jnp.mean(scaled_two, axis=-1, keepdims=True)
    proj_two = jnp.mean(scaled_two * hat_two_local, axis=-1, keepdims=True)
    cot_float = cotangent.astype(jnp.float32)
    d_residual = cot_float + inv_two_local * (scaled_two - mean_two - hat_two_local * proj_two)
    part_two_gain = jnp.sum(d_normed_two * hat_two_local, axis=0)
    part_two_bias = jnp.sum(d_normed_two, axis=0)
    part_up_bias = jnp.sum(d_upper.astype(jnp.float32), axis=0)
    part_down_bias = jnp.sum(cot_float, axis=0)
    grad_attn = lax.all_gather(d_residual.astype(jnp.bfloat16), "gy", axis=0, tiled=True)
    part_output_bias = jnp.sum(d_residual, axis=0)
    d_mixed = dot_right_t(grad_attn, w_output).astype(jnp.bfloat16)
    d_query, d_key, d_value = attend_back(query, key, value, lse, d_mixed)
    grad_query_weight, grad_key_weight, grad_value_weight, grad_output_weight = (
        lax.psum_scatter(
            dot_left_t(normed, d_query).astype(jnp.bfloat16), "gx", scatter_dimension=0, tiled=True
        ).astype(jnp.float32),
        lax.psum_scatter(
            dot_left_t(normed, d_key).astype(jnp.bfloat16), "gx", scatter_dimension=0, tiled=True
        ).astype(jnp.float32),
        lax.psum_scatter(
            dot_left_t(normed, d_value).astype(jnp.bfloat16), "gx", scatter_dimension=0, tiled=True
        ).astype(jnp.float32),
        lax.psum_scatter(
            dot_left_t(mixed, grad_attn).astype(jnp.bfloat16), "gx", scatter_dimension=1, tiled=True
        ).astype(jnp.float32),
    )
    d_normed = lax.psum_scatter(
        (
            dot_right_t(d_query, w_query)
            + dot_right_t(d_key, w_key)
            + dot_right_t(d_value, w_value)
        ).astype(jnp.bfloat16),
        "gy",
        scatter_dimension=0,
        tiled=True,
    ).astype(jnp.float32)
    hat_one_local = lax.dynamic_slice_in_dim(hat_one, start, local, 0)
    inv_one_local = lax.dynamic_slice_in_dim(inv_one, start, local, 0)
    scaled_one = d_normed * gain_one.astype(jnp.float32)
    mean_one = jnp.mean(scaled_one, axis=-1, keepdims=True)
    proj_one = jnp.mean(scaled_one * hat_one_local, axis=-1, keepdims=True)
    grad_input = (
        d_residual + inv_one_local * (scaled_one - mean_one - hat_one_local * proj_one)
    ).astype(jnp.bfloat16)
    part_one_gain = jnp.sum(d_normed * hat_one_local, axis=0)
    part_one_bias = jnp.sum(d_normed, axis=0)
    part_query_bias = jnp.sum(d_query.astype(jnp.float32), axis=0)
    part_value_bias = jnp.sum(d_value.astype(jnp.float32), axis=0)
    feat_one_gain, feat_one_bias, feat_output_bias, feat_two_gain, feat_two_bias, feat_down_bias = (
        lax.psum_scatter(part_one_gain, "gy", scatter_dimension=0, tiled=True),
        lax.psum_scatter(part_one_bias, "gy", scatter_dimension=0, tiled=True),
        lax.psum_scatter(part_output_bias, "gy", scatter_dimension=0, tiled=True),
        lax.psum_scatter(part_two_gain, "gy", scatter_dimension=0, tiled=True),
        lax.psum_scatter(part_two_bias, "gy", scatter_dimension=0, tiled=True),
        lax.psum_scatter(part_down_bias, "gy", scatter_dimension=0, tiled=True),
    )
    (
        grad_one_gain,
        grad_one_bias,
        grad_query_bias,
        grad_value_bias,
        grad_output_bias,
        grad_two_gain,
        grad_two_bias,
        grad_up_bias,
        grad_down_bias,
    ) = lax.psum(
        (
            feat_one_gain,
            feat_one_bias,
            part_query_bias,
            part_value_bias,
            feat_output_bias,
            feat_two_gain,
            feat_two_bias,
            part_up_bias,
            feat_down_bias,
        ),
        "gx",
    )
    return (
        layer_output,
        grad_input,
        grad_one_gain,
        grad_one_bias,
        grad_query_weight,
        grad_query_bias,
        grad_key_weight,
        grad_value_weight,
        grad_value_bias,
        grad_output_weight,
        grad_output_bias,
        grad_two_gain,
        grad_two_bias,
        grad_up_weight,
        grad_up_bias,
        grad_down_weight,
        grad_down_bias,
    )


def solution(mesh):
    return jax.shard_map(
        shards,
        mesh=mesh,
        in_specs=(
            P(("gx", "gy"), None),
            P("gy"),
            P("gy"),
            P("gx", "gy"),
            P("gy"),
            P("gx", "gy"),
            P("gx", "gy"),
            P("gy"),
            P("gy", "gx"),
            P("gy"),
            P("gy"),
            P("gy"),
            P("gx", "gy"),
            P("gy"),
            P("gy", "gx"),
            P("gy"),
            P(("gx", "gy"), None),
        ),
        out_specs=(
            P(("gx", "gy"), None),
            P(("gx", "gy"), None),
            P("gy"),
            P("gy"),
            P("gx", "gy"),
            P("gy"),
            P("gx", "gy"),
            P("gx", "gy"),
            P("gy"),
            P("gy", "gx"),
            P("gy"),
            P("gy"),
            P("gy"),
            P("gx", "gy"),
            P("gy"),
            P("gy", "gx"),
            P("gy"),
        ),
        check_vma=False,
    )
```

profile of v0, /device:TPU:0, one launch (start us, length us, event | category | flops | bytes accessed | tf_op | source)
XLA Modules:
  0.0 1392.4 jit_solution(10019122874200687494)
XLA Ops:
  16.4 39.7 %all-reduce.20 = (bf16[1152]{0:T(1024)(128)(2,1)S(1)}, bf16[1152]{0:T(1024)(128)(2,1)S(1)}, bf16[1152]{0:T(1024)(128)(2,1)S(1)}, bf16[1152]{0:T(1024)(128)(2,1)S...) all-reduce(bf16[1152]{0:T(1024)(128)(2,1)S(1)} %dynamic-update-slic, ...), channel_id=1, replica_groups=mesh['gx'=4,'gy'=8] {'gy'}, use_global_device_ids=true, to_apply=%add.1 | all-reduce | flops 6912 | bytes 27648
  56.1 6.6 all-gather.3
  63.2 7.1 all-gather
  70.7 6.8 all-gather.2
  78.1 6.8 all-gather.1
  85.4 8.0 all-gather.19.cloned.1.call-done
  114.2 18.5 %while.36 = (s32[]{:T(128)}, bf16[2,1024,2,72]{1,3,2,0:T(8,128)(2,1)S(1)}, bf16[2,1024,2,72]{1,3,2,0:T(8,128)(2,1)S(1)}, bf16[2,1024,2,72]{1,3,2,0:T(8,128)(2,1)...) while((s32[]{:T(128)}, bf16[2,1024,2,72]{1,3,2,0:T(8,128)(2,1)S(1)}, ...), condition=%wide.region_5.6_spmd, body=%wide.region_2.5_spmd.sunk | while | flops 614614016 | bytes 17975372 | solution.py:59
  114.2 5.0 fusion.255
  119.2 4.3 fusion.256
  123.5 5.0 fusion.255
  137.3 93.5 %reduce-scatter.20.cloned.1.call-done = bf16[256,1152]{1,0:T(8,128)(2,1)} async-done(((bf16[2048,1152]{1,0:T(8,128)(2,1)}), bf16[256,1152]{1,0:T(8,128)(2,1)}) %reduce-scatter.20.cloned.1.call-update) | async-done | bytes 589840 | tf_op jit(solution)/shard_map/reduce_scatter | solution.py:146
  234.3 78.9 %all-gather.21.cloned.1.call-done = bf16[2048,1152]{1,0:T(8,128)(2,1)} async-done(((bf16[256,1152]{1,0:T(8,128)(2,1)}), bf16[2048,1152]{1,0:T(8,128)(2,1)}) %all-gather.21.cloned.1.call-update) | async-done | bytes 4718608 | tf_op jit(solution)/shard_map/all_gather | solution.py:151
  318.4 13.5 all-gather.23.cloned.1.call-done
  331.9 20.6 %all-gather.25.cloned.1.call-done = bf16[538,1152]{0,1:T(8,128)(2,1)} async-done(((bf16[538,288]{0,1:T(8,128)(2,1)}), bf16[538,1152]{0,1:T(8,128)(2,1)}) %all-gather.25.cloned.1.call-update) | async-done | bytes 1239568 | tf_op jit(solution)/shard_map/all_gather | solution.py:129
  352.4 12.9 convolution_convert_fusion.2
  365.6 95.5 %reduce-scatter.22.cloned.1.call-done = bf16[256,1152]{1,0:T(8,128)(2,1)} async-done(((bf16[2048,1152]{1,0:T(8,128)(2,1)}), bf16[256,1152]{1,0:T(8,128)(2,1)}) %reduce-scatter.22.cloned.1.call-update) | async-done | bytes 589840 | tf_op jit(solution)/shard_map/reduce_scatter | solution.py:163
  464.6 37.2 %all-reduce.19 = (bf16[1152]{0:T(1024)(128)(2,1)}, bf16[1152]{0:T(1024)(128)(2,1)}, bf16[1152]{0:T(1024)(128)(2,1)S(1)}, bf16[1152]{0:T(1024)(128)(2,1)S(1)}, bf16[1152]{0:T(1024)(128)(2,1)}) all-reduce(bf16[1152]{0:T(1024)(128)(2,1)S(1)} %dynamic-update-slice.10, ...), channel_id=1, replica_groups=mesh['gx'=4,'gy'=8] {'gy'}, use_global_device_ids=true, to_apply=%add.10 | all-reduce | flops 5760 | bytes 23040
  501.9 6.5 all-gather.4
  508.9 6.8 all-gather.5
  516.2 6.8 all-gather.6
  523.5 7.3 all-gather.7
  532.1 11.5 all-gather.27.cloned.1.call-done
  548.7 4.6 fusion.97
  567.0 9.2 while.37
  577.1 4.8 convolution_convert_fusion.1
  582.5 92.9 %reduce-scatter.24.cloned.1.call-done = bf16[256,1152]{1,0:T(8,128)(2,1)} async-done(((bf16[2048,1152]{1,0:T(8,128)(2,1)}), bf16[256,1152]{1,0:T(8,128)(2,1)}) %reduce-scatter.24.cloned.1.call-update) | async-done | bytes 589840 | tf_op jit(solution)/shard_map/reduce_scatter | solution.py:146
  679.5 78.4 %all-gather.29.cloned.1.call-done = bf16[2048,1152]{1,0:T(8,128)(2,1)} async-done(((bf16[256,1152]{1,0:T(8,128)(2,1)}), bf16[2048,1152]{1,0:T(8,128)(2,1)}) %all-gather.29.cloned.1.call-update) | async-done | bytes 4718608 | tf_op jit(solution)/shard_map/all_gather | solution.py:151
  763.1 13.5 all-gather.35.cloned.1.call-done
  776.6 8.4 fusion.153
  785.0 73.7 %all-gather.33.cloned.1.call-done = bf16[2048,1152]{1,0:T(8,128)(2,1)} async-done(((bf16[256,1152]{1,0:T(8,128)(2,1)}), bf16[2048,1152]{1,0:T(8,128)(2,1)}) %all-gather.33.cloned.1.call-update) | async-done | bytes 4718608 | tf_op jit(solution)/shard_map/all_gather | solution.py:260
  858.7 18.7 %all-gather.31.cloned.1.call-done = bf16[538,1152]{0,1:T(8,128)(2,1)} async-done(((bf16[538,288]{0,1:T(8,128)(2,1)}), bf16[538,1152]{0,1:T(8,128)(2,1)}) %all-gather.31.cloned.1.call-update) | async-done | bytes 1239568 | tf_op jit(solution)/shard_map/all_gather | solution.py:129
  877.4 10.6 convert_reduce_fusion.4
  889.4 7.5 convolution_convert_fusion
  897.6 5.9 fusion.99
  903.5 88.8 %reduce-scatter.26.cloned.1.call-done = bf16[256,1152]{1,0:T(8,128)(2,1)} async-done(((bf16[2048,1152]{1,0:T(8,128)(2,1)}), bf16[256,1152]{1,0:T(8,128)(2,1)}) %reduce-scatter.26.cloned.1.call-update) | async-done | bytes 589840 | tf_op jit(solution)/shard_map/reduce_scatter | solution.py:278
  998.3 9.1 convolution_convert_fusion.4
  1007.9 8.9 convolution_convert_fusion.5
  1016.9 61.1 %all-gather.37.cloned.1.call-done = bf16[2048,1152]{1,0:T(8,128)(2,1)} async-done(((bf16[256,1152]{1,0:T(8,128)(2,1)}), bf16[2048,1152]{1,0:T(8,128)(2,1)}) %all-gather.37.cloned.1.call-update) | async-done | bytes 4718608 | tf_op jit(solution)/shard_map/all_gather | solution.py:292
  1078.0 4.8 convolution_convert_fusion.10
  1095.1 21.3 %while.38 = (s32[]{:T(128)}, bf16[2,1024,2,72]{1,3,2,0:T(8,128)(2,1)}, bf16[2,1024,2,72]{1,3,2,0:T(8,128)(2,1)}, bf16[2,1024,2,72]{1,3,2,0:T(8,128)(2,1)S(1)}, b...) while((s32[]{:T(128)}, ...), condition=%wide.region_24.25_spmd, body=%wide.region_22.24_spmd.sunk | while | flops 1535850496 | bytes 77722880 | solution.py:90
  1137.0 6.2 fusion.188
  1143.3 5.7 convolution_add_fusion.1
  1162.5 22.7 %reduce-scatter.34.cloned.1.call-done = bf16[288,144]{1,0:T(8,128)(2,1)} async-done(((bf16[1152,144]{1,0:T(8,128)(2,1)}), bf16[288,144]{1,0:T(8,128)(2,1)}) %reduce-scatter.34.cloned.1.call-update) | async-done | bytes 82960
  1187.0 22.9 %reduce-scatter.36.cloned.1.call-done = bf16[288,144]{1,0:T(8,128)(2,1)} async-done(((bf16[1152,144]{1,0:T(8,128)(2,1)}), bf16[288,144]{1,0:T(8,128)(2,1)}) %reduce-scatter.36.cloned.1.call-update) | async-done | bytes 82960
  1211.6 22.7 %reduce-scatter.38.cloned.1.call-done = bf16[288,144]{1,0:T(8,128)(2,1)} async-done(((bf16[1152,144]{1,0:T(8,128)(2,1)}), bf16[288,144]{1,0:T(8,128)(2,1)}) %reduce-scatter.38.cloned.1.call-update) | async-done | bytes 82960
  1236.0 97.2 %reduce-scatter.28.cloned.1.call-done = bf16[256,1152]{1,0:T(8,128)(2,1)} async-done(((bf16[2048,1152]{1,0:T(8,128)(2,1)}), bf16[256,1152]{1,0:T(8,128)(2,1)}) %reduce-scatter.28.cloned.1.call-update) | async-done | bytes 589840 | tf_op jit(solution)/shard_map/reduce_scatter | solution.py:310
  1335.2 36.4 %all-reduce.17 = (f32[1152]{0:T(1024)S(1)}, f32[1152]{0:T(1024)S(1)}, f32[1152]{0:T(1024)S(1)}, f32[1152]{0:T(1024)S(1)}, f32[1152]{0:T(1024)S(1)}, /*index=5*/f32[1152]{0:T(1024)S(1)}) all-reduce(f32[1152]{0:T(1024)S(1)} %get-tuple-element.226, f32[1152]{0:T(1024)S(1)} %get-tuple-element.231, ...), channel_id=7, replica_groups=mesh['gx'=4,'gy'=8] {'gy'}, use_global_device_ids=true, to_apply=%region_29.30.clone | all-reduce | flops 6912 | bytes 55296
  1372.1 10.7 all-reduce.18
  (344 shorter events, 178.5 us)
Async XLA Ops:
  7.2 86.2 %all-gather.19.cloned.1.call-start = ((), (), s32[]{:S(2)}) async-start(), calls=%async_computation.11 | async-start | bytes 5308416 | tf_op jit(solution)/shard_map/all_gather | solution.py:132
  7.9 222.8 %reduce-scatter.20.cloned.1.call-start = ((), (), s32[]{:S(2)}) async-start(), calls=%async_computation.12 | async-start | bytes 5308416 | tf_op jit(solution)/shard_map/reduce_scatter | solution.py:146
  137.2 97.1 %copy-start.40 = (bf16[538]{0:T(1024)(128)(2,1)S(1)}, bf16[538]{0:T(1024)(128)(2,1)}, u32[]{:S(2)}) copy-start(bf16[538]{0:T(1024)(128)(2,1)} %param.36) | copy-start | bytes 3232
  137.2 176.0 %all-gather.21.cloned.1.call-start = ((), (), s32[]{:S(2)}) async-start(), calls=%async_computation.13 | async-start | bytes 5308416 | tf_op jit(solution)/shard_map/all_gather | solution.py:151
  232.9 99.0 %all-gather.23.cloned.1.call-start = ((), (), s32[]{:S(2)}) async-start(), calls=%async_computation.14 | async-start | bytes 1843200 | tf_op jit(solution)/shard_map/all_gather | solution.py:128
  233.4 119.0 %all-gather.25.cloned.1.call-start = ((), (), s32[]{:S(2)}) async-start(), calls=%async_computation.15 | async-start | bytes 1843200 | tf_op jit(solution)/shard_map/all_gather | solution.py:129
  234.0 227.0 %reduce-scatter.22.cloned.1.call-start = ((), (), s32[]{:S(2)}) async-start(), calls=%async_computation.16 | async-start | bytes 5308416 | tf_op jit(solution)/shard_map/reduce_scatter | solution.py:163
  365.4 95.7 %copy-start.13 = (bf16[256,1152]{1,0:T(8,128)(2,1)S(1)}, bf16[256,1152]{1,0:T(8,128)(2,1)}, u32[]{:S(2)}) copy-start(bf16[256,1152]{1,0:T(8,128)(2,1)} %reduce-scatter.20.cloned.1.call-done) | copy-start | bytes 1769476
  365.4 97.9 %copy-start.49 = (bf16[144]{0:T(256)(128)(2,1)S(1)}, bf16[144]{0:T(256)(128)(2,1)}, u32[]{:S(2)}) copy-start(bf16[144]{0:T(256)(128)(2,1)} %param.30) | copy-start | bytes 868
  365.4 97.9 %copy-start.50 = (bf16[144]{0:T(256)(128)(2,1)S(1)}, bf16[144]{0:T(256)(128)(2,1)}, u32[]{:S(2)}) copy-start(bf16[144]{0:T(256)(128)(2,1)} %param.27) | copy-start | bytes 868
  365.4 98.0 %copy-start.51 = (bf16[144]{0:T(256)(128)(2,1)S(1)}, bf16[144]{0:T(256)(128)(2,1)}, u32[]{:S(2)}) copy-start(bf16[144]{0:T(256)(128)(2,1)} %param.34) | copy-start | bytes 868
  365.4 98.2 %copy-start.52 = (bf16[144]{0:T(256)(128)(2,1)S(1)}, bf16[144]{0:T(256)(128)(2,1)}, u32[]{:S(2)}) copy-start(bf16[144]{0:T(256)(128)(2,1)} %param.33) | copy-start | bytes 868
  365.4 98.5 %copy-start.53 = (bf16[144]{0:T(256)(128)(2,1)S(1)}, bf16[144]{0:T(256)(128)(2,1)}, u32[]{:S(2)}) copy-start(bf16[144]{0:T(256)(128)(2,1)} %param.32) | copy-start | bytes 868
  365.4 98.7 %copy-start.54 = (bf16[144]{0:T(256)(128)(2,1)S(1)}, bf16[144]{0:T(256)(128)(2,1)}, u32[]{:S(2)}) copy-start(bf16[144]{0:T(256)(128)(2,1)} %param.25) | copy-start | bytes 868
  365.4 99.0 %copy-start.55 = (bf16[144]{0:T(256)(128)(2,1)S(1)}, bf16[144]{0:T(256)(128)(2,1)}, u32[]{:S(2)}) copy-start(bf16[144]{0:T(256)(128)(2,1)} %param.24) | copy-start | bytes 868
  365.4 136.4 %copy-start.23 = (bf16[288,144]{0,1:T(8,128)(2,1)S(1)}, bf16[288,144]{0,1:T(8,128)(2,1)}, u32[]{:S(2)}) copy-start(bf16[288,144]{0,1:T(8,128)(2,1)} %param.29) | copy-start | bytes 248836
  365.5 178.0 %all-gather.27.cloned.1.call-start = ((), (), s32[]{:S(2)}) async-start(), calls=%async_computation.17 | async-start | bytes 5308416 | tf_op jit(solution)/shard_map/all_gather | solution.py:132
  365.5 158.0 %copy-start.26 = (bf16[144,288]{1,0:T(8,128)(2,1)S(1)}, bf16[144,288]{1,0:T(8,128)(2,1)}, u32[]{:S(2)}) copy-start(bf16[144,288]{1,0:T(8,128)(2,1)} %param.31) | copy-start | bytes 248836
  463.2 212.2 %reduce-scatter.24.cloned.1.call-start = ((), (), s32[]{:S(2)}) async-start(), calls=%async_computation.18 | async-start | bytes 5308416 | tf_op jit(solution)/shard_map/reduce_scatter | solution.py:146
  581.9 93.6 %copy-start.6 = (bf16[256,1152]{1,0:T(8,128)(2,1)S(1)}, bf16[256,1152]{1,0:T(8,128)(2,1)}, u32[]{:S(2)}) copy-start(bf16[256,1152]{1,0:T(8,128)(2,1)} %param.23) | copy-start | bytes 1769476
  581.9 97.0 %copy-start.46 = (bf16[1152]{0:T(1024)(128)(2,1)S(1)}, bf16[1152]{0:T(1024)(128)(2,1)}, u32[]{:S(2)}) copy-start(bf16[1152]{0:T(1024)(128)(2,1)} %get-tuple-element.287) | copy-start | bytes 6916
  581.9 97.1 %copy-start.41 = (bf16[538]{0:T(1024)(128)(2,1)S(1)}, bf16[538]{0:T(1024)(128)(2,1)}, u32[]{:S(2)}) copy-start(bf16[538]{0:T(1024)(128)(2,1)} %param.36) | copy-start | bytes 3232
  581.9 97.1 %copy-start.45 = (bf16[1152]{0:T(1024)(128)(2,1)S(1)}, bf16[1152]{0:T(1024)(128)(2,1)}, u32[]{:S(2)}) copy-start(bf16[1152]{0:T(1024)(128)(2,1)} %get-tuple-element.288) | copy-start | bytes 6916
  581.9 176.0 %all-gather.29.cloned.1.call-start = ((), (), s32[]{:S(2)}) async-start(), calls=%async_computation.19 | async-start | bytes 5308416 | tf_op jit(solution)/shard_map/all_gather | solution.py:151
  677.5 99.0 %all-gather.35.cloned.1.call-start = ((), (), s32[]{:S(2)}) async-start(), calls=%async_computation.22 | async-start | bytes 1843200 | tf_op jit(solution)/shard_map/all_gather | solution.py:128
  678.1 180.6 %all-gather.33.cloned.1.call-start = ((), (), s32[]{:S(2)}) async-start(), calls=%async_computation.21 | async-start | bytes 5308416 | tf_op jit(solution)/shard_map/all_gather | solution.py:260
  678.9 198.5 %all-gather.31.cloned.1.call-start = ((), (), s32[]{:S(2)}) async-start(), calls=%async_computation.20 | async-start | bytes 1843200 | tf_op jit(solution)/shard_map/all_gather | solution.py:129
  678.9 97.6 %copy-start.42 = (f32[1152]{0:T(1024)}, f32[1152]{0:T(1024)S(1)}, u32[]{:S(2)}) copy-start(f32[1152]{0:T(1024)S(1)} %convert_element_type.291) | copy-start | bytes 13828
  679.0 198.4 %copy-start.48 = (f32[538]{0:T(1024)}, f32[538]{0:T(1024)S(1)}, u32[]{:S(2)}) copy-start(f32[538]{0:T(1024)S(1)} %convert_element_type.293) | copy-start | bytes 6460
  679.0 313.3 %copy-start.29 = (f32[1152]{0:T(1024)}, f32[1152]{0:T(1024)S(1)}, u32[]{:S(2)}) copy-start(f32[1152]{0:T(1024)S(1)} %convert_element_type.290) | copy-start | bytes 13828
  679.4 312.9 %reduce-scatter.26.cloned.1.call-start = ((), (), s32[]{:S(2)}) async-start(), calls=%async_computation.23 | async-start | bytes 5308416 | tf_op jit(solution)/shard_map/reduce_scatter | solution.py:278
  761.6 136.0 %copy-start.31 = (f32[2048]{0:T(1024)}, f32[2048]{0:T(1024)S(1)}, u32[]{:S(2)}) copy-start(f32[2048]{0:T(1024)S(1)} %broadcast_multiply_fusion) | copy-start | bytes 24580
  763.1 134.5 %copy-start.34 = (f32[2048]{0:T(1024)}, f32[2048]{0:T(1024)S(1)}, u32[]{:S(2)}) copy-start(f32[2048]{0:T(1024)S(1)} %add_rsqrt_fusion) | copy-start | bytes 24580
  896.9 181.1 %all-gather.37.cloned.1.call-start = ((), (), s32[]{:S(2)}) async-start(), calls=%async_computation.24 | async-start | bytes 5308416 | tf_op jit(solution)/shard_map/all_gather | solution.py:292
  897.6 97.2 %copy-start.17 = (bf16[256,1152]{1,0:T(8,128)(2,1)S(1)}, bf16[256,1152]{1,0:T(8,128)(2,1)}, u32[]{:S(2)}) copy-start(bf16[256,1152]{1,0:T(8,128)(2,1)} %param.39) | copy-start | bytes 1769476
  998.3 156.1 %reduce-scatter.32.cloned.1.call-start = ((), (), s32[]{:S(2)}) async-start(), calls=%async_computation.27 | async-start | bytes 1843200 | tf_op jit(solution)/shard_map/reduce_scatter | solution.py:271
  1007.4 148.9 %reduce-scatter.30.cloned.1.call-start = ((), (), s32[]{:S(2)}) async-start(), calls=%async_computation.26 | async-start | bytes 1843200 | tf_op jit(solution)/shard_map/reduce_scatter | solution.py:265
  1016.9 143.9 %reduce-scatter.40.cloned.1.call-start = ((), (), s32[]{:S(2)}) async-start(), calls=%async_computation.31 | async-start | bytes 737280
  1093.1 92.1 %reduce-scatter.34.cloned.1.call-start = ((), (), s32[]{:S(2)}) async-start(), calls=%async_computation.28 | async-start | bytes 737280
  1122.7 87.1 %reduce-scatter.36.cloned.1.call-start = ((), (), s32[]{:S(2)}) async-start(), calls=%async_computation.29 | async-start | bytes 737280
  1130.6 103.7 %reduce-scatter.38.cloned.1.call-start = ((), (), s32[]{:S(2)}) async-start(), calls=%async_computation.30 | async-start | bytes 737280
  1143.2 190.0 %reduce-scatter.28.cloned.1.call-start = ((), (), s32[]{:S(2)}) async-start(), calls=%async_computation.25 | async-start | bytes 5308416 | tf_op jit(solution)/shard_map/reduce_scatter | solution.py:310
  1152.8 180.4 %copy-start.28 = (f32[1152]{0:T(1024)S(1)}, f32[1152]{0:T(1024)}, u32[]{:S(2)}) copy-start(f32[1152]{0:T(1024)} %copy-done.27) | copy-start | bytes 13828
  1152.8 182.3 %copy-start.36 = (f32[1152]{0:T(1024)S(1)}, f32[1152]{0:T(1024)}, u32[]{:S(2)}) copy-start(f32[1152]{0:T(1024)} %get-tuple-element.224) | copy-start | bytes 13828
  1152.8 182.3 %copy-start.37 = (f32[1152]{0:T(1024)S(1)}, f32[1152]{0:T(1024)}, u32[]{:S(2)}) copy-start(f32[1152]{0:T(1024)} %get-tuple-element.230) | copy-start | bytes 13828
  1152.9 182.3 %copy-start.38 = (f32[1152]{0:T(1024)S(1)}, f32[1152]{0:T(1024)}, u32[]{:S(2)}) copy-start(f32[1152]{0:T(1024)} %get-tuple-element.298) | copy-start | bytes 13828
  1152.9 182.3 %copy-start.39 = (f32[1152]{0:T(1024)S(1)}, f32[1152]{0:T(1024)}, u32[]{:S(2)}) copy-start(f32[1152]{0:T(1024)} %get-tuple-element.308) | copy-start | bytes 13828
  1152.9 219.2 %copy-start.44 = (f32[538]{0:T(1024)S(1)}, f32[538]{0:T(1024)}, u32[]{:S(2)}) copy-start(f32[538]{0:T(1024)} %get-tuple-element.311) | copy-start | bytes 6460
  (35 other events, 568.1 us)
Sparse Core Ops, SparseCore 0:
  10.2 83.0 all-gather.18
  137.4 93.3 reduce-scatter.19
  233.5 79.6 all-gather.20
  314.6 17.2 all-gather.22
  333.3 19.1 all-gather.24
  365.6 95.3 reduce-scatter.21
  463.4 80.1 all-gather.26
  582.0 93.3 reduce-scatter.23
  678.2 79.6 all-gather.28
  759.3 17.2 all-gather.34
  778.8 79.8 all-gather.32
  860.1 17.2 all-gather.30
  897.0 95.2 reduce-scatter.25
  998.3 79.6 all-gather.36
  1080.4 25.6 reduce-scatter.31
  1108.8 27.5 reduce-scatter.29
  1138.7 22.0 reduce-scatter.39
  1163.2 22.0 reduce-scatter.33
  1187.7 22.0 reduce-scatter.35
  1212.2 22.0 reduce-scatter.37
  1238.0 95.2 reduce-scatter.27
where the time goes:
time: 1400 us; the launch traced here: 1390 us
  waiting for transfers between devices  920 us (66%)
  blocking collectives  179 us (13%)
  matrix products  161 us (12%)
  other arithmetic  63.7 us (5%)
  local copies, waits for them, and re-layouts  50.3 us (4%)
  between operations  17 us (1%)
    reduce_scatter x2, waiting for transfers between devices, forward_pass(): lax.psum_scatter(dot_plain(mixed, w_output).astype(jnp.bfloat16), 'gy', s...  186 us
    all_gather x2, waiting for transfers between devices, forward_pass(): lax.all_gather(residual.astype(jnp.bfloat16), 'gy', axis=0, tiled=True)  157 us
    unnamed x3, blocking collectives  113 us
    reduce_scatter x1, waiting for transfers between devices, shards(): lax.psum_scatter((dot_right_t(d_query, w_query) + dot_right_t(d_key, w_ke...  97.2 us
    reduce_scatter x1, waiting for transfers between devices, forward_pass(): lax.psum_scatter(dot_plain(active, w_down).astype(jnp.bfloat16), 'gy', sc...  95.5 us
    reduce_scatter x1, waiting for transfers between devices, shards(): lax.psum_scatter(dot_right_t(d_upper, w_up).astype(jnp.bfloat16), 'gy', s...  88.8 us
    unnamed x25, waiting for transfers between devices  74 us
    all_gather x1, waiting for transfers between devices, shards(): grad_rows = lax.all_gather(cotangent, 'gy', axis=0, tiled=True)  73.7 us
  transfers between devices with their start and end apart: 21, of which 19 were waited for; matrix products, arithmetic and copies ran while one was open for 10% of the time, Pallas kernels for 0%

commit v1 on v0

--- a/solution.py
+++ b/solution.py
@@ -2,6 +2,7 @@
 import jax.numpy as jnp
 from jax import lax
 from jax.sharding import PartitionSpec as P
+from jax.lax import axis_index, axis_size, ppermute
 
 HD = 72
 LENGTH = 1024
@@ -147,8 +148,34 @@
         dot_plain(mixed, w_output).astype(jnp.bfloat16), "gy", scatter_dimension=0, tiled=True
     ).astype(jnp.float32)
     residual = layer_input.astype(jnp.float32) + attn_part + out_shift.astype(jnp.float32)
+
+    def extend_sites_here(panel, pos_dim):
+        a_name = "gy"
+        mat_out = axis_index(a_name)
+        t1 = axis_size(a_name)
+        s_next, block_now, low = (t1, mat_out, panel.shape[pos_dim])
+        inbox = [(s, (s + 1) % s_next) for s in range(s_next)]
+        opened = jnp.zeros(
+            (*panel.shape[:pos_dim], s_next * low, *panel.shape[pos_dim + 1 :]), panel.dtype
+        )
+        opened = lax.dynamic_update_slice_in_dim(opened, panel, block_now * low, axis=pos_dim)
+        items = [(s, (s - 1) % s_next) for s in range(s_next)]
+        x_next = s_next // 2
+        wide_out = arr_next = panel
+        for kk in [*range(1, x_next + 1)]:
+            wide_out = ppermute(wide_out, a_name, perm=inbox)
+            opened = lax.dynamic_update_slice_in_dim(
+                opened, wide_out, (block_now - kk) % s_next * low, axis=pos_dim
+            )
+            if kk < s_next - x_next:
+                arr_next = ppermute(arr_next, axis_name=a_name, perm=items)
+                opened = lax.dynamic_update_slice_in_dim(
+                    opened, arr_next, (block_now + kk) % s_next * low, axis=pos_dim
+                )
+        return opened
+
     rows_two, gain_two, shift_two = (
-        lax.all_gather(residual.astype(jnp.bfloat16), "gy", axis=0, tiled=True),
+        extend_sites_here(residual.astype(jnp.bfloat16), 0),
         lax.all_gather(norm_two_gain, "gy", axis=0, tiled=True),
         lax.all_gather(norm_two_bias, "gy", axis=0, tiled=True),
     )

time: 1400 us -> 1330 us (0.950)
  waiting for transfers between devices: 920 us -> 796 us
  starting transfers between devices: 1.86 us -> 35.4 us
  local copies, waits for them, and re-layouts: 50.3 us -> 64.3 us
    all_gather x2 -> x0, waiting for transfers between devices: 157 us -> none  [forward_pass(): lax.all_gather(residual.astype(jnp.bfloat16), 'gy', axis=0, tiled=True)]
    ppermute x0 -> x14, waiting for transfers between devices: none -> 138 us  [the longest x8 138 us: extend_sites_here(): wide_out = ppermute(wide_out, a_name, perm=inbox)]
    all_gather x1, waiting for transfers between devices: 73.7 us -> 0.01 us  [shards(): grad_rows = lax.all_gather(cotangent, 'gy', axis=0, tiled=True)]
    all_gather x2, waiting for transfers between devices: 39.2 us -> 0.02 us  [forward_pass(): lax.all_gather(down_weight, 'gx', axis=1, tiled=True)]
    reduce_scatter x2, waiting for transfers between devices: 186 us -> 222 us  [forward_pass(): lax.psum_scatter(dot_plain(mixed, w_output).astype(jnp.bfloat16), 'gy', s...]
    ppermute x0 -> x14, starting transfers between devices: none -> 34.1 us  [the longest x8 18.1 us: extend_sites_here(): wide_out = ppermute(wide_out, a_name, perm=inbox)]
    all_gather x2, waiting for transfers between devices: 27 us -> 0.05 us  [forward_pass(): lax.all_gather(up_weight, 'gx', axis=0, tiled=True)]
    unnamed x154 -> x158, local copies, waits for them, and re-layouts: 32.1 us -> 28.5 us
  transfers between devices with their start and end apart: 21 -> 33, of which waited for: 19 -> 20; matrix products, arithmetic and copies ran while one was open for 10% -> 13% of each run, Pallas kernels for 0% -> 0%
where the time goes in v1:
time: 1330 us
  waiting for transfers between devices  796 us (60%)
  blocking collectives  179 us (13%)
  matrix products  160 us (12%)
  other arithmetic  73.6 us (6%)
  local copies, waits for them, and re-layouts  64.3 us (5%)
  starting transfers between devices  35.4 us (3%)
  between operations  18.7 us (1%)
    reduce_scatter x2, waiting for transfers between devices, forward_pass(): lax.psum_scatter(dot_plain(mixed, w_output).astype(jnp.bfloat16), 'gy', s...  222 us
    ppermute x8, waiting for transfers between devices, extend_sites_here(): wide_out = ppermute(wide_out, a_name, perm=inbox)  138 us
    unnamed x3, blocking collectives  114 us
    reduce_scatter x1, waiting for transfers between devices, shards(): lax.psum_scatter((dot_right_t(d_query, w_query) + dot_right_t(d_key, w_ke...  97.1 us
    reduce_scatter x1, waiting for transfers between devices, forward_pass(): lax.psum_scatter(dot_plain(active, w_down).astype(jnp.bfloat16), 'gy', sc...  95.1 us
    reduce_scatter x1, waiting for transfers between devices, shards(): lax.psum_scatter(dot_right_t(d_upper, w_up).astype(jnp.bfloat16), 'gy', s...  87.1 us
    unnamed x23, waiting for transfers between devices  76.1 us
    all_gather x1, waiting for transfers between devices, shards(): lax.all_gather(d_residual.astype(jnp.bfloat16), 'gy', axis=0, tiled=True)  61 us
  transfers between devices with their start and end apart: 33, of which 20 were waited for; matrix products, arithmetic and copies ran while one was open for 13% of the time, Pallas kernels for 0%

profile of v1, /device:TPU:0, one launch (start us, length us, event | category | flops | bytes accessed | tf_op | source)
XLA Modules:
  0.0 1327.3 jit_solution(17789943679727513312)
XLA Ops:
  15.9 40.3 %all-reduce.20 = (bf16[1152]{0:T(1024)(128)(2,1)S(1)}, bf16[1152]{0:T(1024)(128)(2,1)S(1)}, bf16[1152]{0:T(1024)(128)(2,1)S(1)}, bf16[1152]{0:T(1024)(128)(2,1)}...) all-reduce(bf16[1152]{0:T(1024)(128)(2,1)S(1)} %dynamic-update-slice.1, ...), channel_id=1, replica_groups=mesh['gx'=4,'gy'=8] {'gy'}, use_global_device_ids=true, to_apply=%add.1 | all-reduce | flops 6912 | bytes 27648
  56.2 6.7 all-gather
  64.1 7.0 all-gather.1
  71.7 6.8 all-gather.2
  79.0 6.8 all-gather.3
  86.3 7.8 all-gather.17.cloned.1.call-done
  115.0 18.6 %while.36 = (s32[]{:T(128)}, bf16[2,1024,2,72]{1,3,2,0:T(8,128)(2,1)S(1)}, bf16[2,1024,2,72]{1,3,2,0:T(8,128)(2,1)S(1)}, bf16[2,1024,2,72]{1,3,2,0:T(8,128)(2,1)...) while((s32[]{:T(128)}, bf16[2,1024,2,72]{1,3,2,0:T(8,128)(2,1)S(1)}, ...), condition=%wide.region_5.6_spmd, body=%wide.region_2.5_spmd.sunk | while | flops 614614016 | bytes 17975364 | solution.py:60
  115.1 5.0 fusion.256
  124.4 5.0 fusion.256
  138.9 92.9 %reduce-scatter.20.cloned.1.call-done = bf16[256,1152]{1,0:T(8,128)(2,1)} async-done(((bf16[2048,1152]{1,0:T(8,128)(2,1)}), bf16[256,1152]{1,0:T(8,128)(2,1)}) %reduce-scatter.20.cloned.1.call-update) | async-done | bytes 589840 | tf_op jit(solution)/shard_map/reduce_scatter | solution.py:147
  240.0 22.0 %collective-permute-done = bf16[256,1152]{1,0:T(8,128)(2,1)S(1)} collective-permute-done((bf16[256,1152]{1,0:T(8,128)(2,1)S(1)}, bf16[256,1152]{1,0:T(8,128)(2,1)S(1)}, u32[]{:S(2)}, u32[]{:S(2)}) %collective-permute-start) | collective-permute-done | bytes 589856 | tf_op jit(solution)/shard_map/ppermute | solution.py:166
  270.1 18.7 %collective-permute-done.2 = bf16[256,1152]{1,0:T(8,128)(2,1)S(1)} collective-permute-done((bf16[256,1152]{1,0:T(8,128)(2,1)S(1)}, bf16[256,1152]{1,0:T(8,128)(2,1)S(1)}, u32[]{:S(2)}, u32[]{:S(2)}) %collective-permute-start.2) | collective-permute-done | bytes 589856 | tf_op jit(solution)/shard_map/ppermute | solution.py:166
  296.2 18.7 %collective-permute-done.4 = bf16[256,1152]{1,0:T(8,128)(2,1)S(1)} collective-permute-done((bf16[256,1152]{1,0:T(8,128)(2,1)S(1)}, bf16[256,1152]{1,0:T(8,128)(2,1)S(1)}, u32[]{:S(2)}, u32[]{:S(2)}) %collective-permute-start.4) | collective-permute-done | bytes 589856 | tf_op jit(solution)/shard_map/ppermute | solution.py:166
  320.4 10.4 collective-permute-done.6
  338.6 13.0 convolution_convert_fusion.2
  351.7 95.1 %reduce-scatter.22.cloned.1.call-done = bf16[256,1152]{1,0:T(8,128)(2,1)} async-done(((bf16[2048,1152]{1,0:T(8,128)(2,1)}), bf16[256,1152]{1,0:T(8,128)(2,1)}) %reduce-scatter.22.cloned.1.call-update) | async-done | bytes 589840 | tf_op jit(solution)/shard_map/reduce_scatter | solution.py:190
  450.4 37.2 %all-reduce.19 = (bf16[1152]{0:T(1024)(128)(2,1)}, bf16[1152]{0:T(1024)(128)(2,1)}, bf16[1152]{0:T(1024)(128)(2,1)S(1)}, bf16[1152]{0:T(1024)(128)(2,1)S(1)}, bf16[1152]{0:T(1024)(128)(2,1)}) all-reduce(bf16[1152]{0:T(1024)(128)(2,1)S(1)} %dynamic-update-slice.10, ...), channel_id=1, replica_groups=mesh['gx'=4,'gy'=8] {'gy'}, use_global_device_ids=true, to_apply=%add.10 | all-reduce | flops 5760 | bytes 23040
  487.6 6.5 all-gather.6
  494.6 6.8 all-gather.5
  502.0 6.8 all-gather.4
  509.4 7.0 all-gather.7
  517.6 11.7 all-gather.23.cloned.1.call-done
  534.5 4.7 fusion.97
  552.8 9.4 while.37
  563.1 4.8 convolution_convert_fusion.1
  569.3 129.3 %reduce-scatter.24.cloned.1.call-done = bf16[256,1152]{1,0:T(8,128)(2,1)} async-done(((bf16[2048,1152]{1,0:T(8,128)(2,1)}), bf16[256,1152]{1,0:T(8,128)(2,1)}) %reduce-scatter.24.cloned.1.call-update) | async-done | bytes 589840 | tf_op jit(solution)/shard_map/reduce_scatter | solution.py:147
  706.8 21.6 %collective-permute-done.7 = bf16[256,1152]{1,0:T(8,128)(2,1)S(1)} collective-permute-done((bf16[256,1152]{1,0:T(8,128)(2,1)S(1)}, bf16[256,1152]{1,0:T(8,128)(2,1)S(1)}, u32[]{:S(2)}, u32[]{:S(2)}) %collective-permute-start.7) | collective-permute-done | bytes 589856 | tf_op jit(solution)/shard_map/ppermute | solution.py:166
  737.1 17.9 %collective-permute-done.9 = bf16[256,1152]{1,0:T(8,128)(2,1)S(1)} collective-permute-done((bf16[256,1152]{1,0:T(8,128)(2,1)S(1)}, bf16[256,1152]{1,0:T(8,128)(2,1)S(1)}, u32[]{:S(2)}, u32[]{:S(2)}) %collective-permute-start.9) | collective-permute-done | bytes 589856 | tf_op jit(solution)/shard_map/ppermute | solution.py:166
  763.8 17.3 %collective-permute-done.11 = bf16[256,1152]{1,0:T(8,128)(2,1)S(1)} collective-permute-done((bf16[256,1152]{1,0:T(8,128)(2,1)S(1)}, bf16[256,1152]{1,0:T(8,128)(2,1)S(1)}, u32[]{:S(2)}, u32[]{:S(2)}) %collective-permute-start.11) | collective-permute-done | bytes 589856 | tf_op jit(solution)/shard_map/ppermute | solution.py:166
  786.2 11.0 collective-permute-done.13
  805.0 8.5 fusion.153
  813.4 10.6 convert_reduce_fusion.4
  825.4 7.4 convolution_convert_fusion
  833.5 5.9 fusion.99
  839.5 87.1 %reduce-scatter.26.cloned.1.call-done = bf16[256,1152]{1,0:T(8,128)(2,1)} async-done(((bf16[2048,1152]{1,0:T(8,128)(2,1)}), bf16[256,1152]{1,0:T(8,128)(2,1)}) %reduce-scatter.26.cloned.1.call-update) | async-done | bytes 589840 | tf_op jit(solution)/shard_map/reduce_scatter | solution.py:305
  932.6 9.1 convolution_convert_fusion.4
  941.9 8.8 convolution_convert_fusion.5
  950.8 61.0 %all-gather.31.cloned.1.call-done = bf16[2048,1152]{1,0:T(8,128)(2,1)} async-done(((bf16[256,1152]{1,0:T(8,128)(2,1)}), bf16[2048,1152]{1,0:T(8,128)(2,1)}) %all-gather.31.cloned.1.call-update) | async-done | bytes 4718608 | tf_op jit(solution)/shard_map/all_gather | solution.py:319
  1025.9 22.7 %while.38 = (s32[]{:T(128)}, bf16[2,1024,2,72]{1,3,2,0:T(8,128)(2,1)}, bf16[2,1024,2,72]{1,3,2,0:T(8,128)(2,1)}, bf16[2,1024,2,72]{1,3,2,0:T(8,128)(2,1)}, bf16[...) while((s32[]{:T(128)}, ...), condition=%wide.region_24.25_spmd, body=%wide.region_22.24_spmd.sunk | while | flops 1535850496 | bytes 75363544 | solution.py:91
  1067.4 6.2 fusion.189
  1073.7 5.4 convolution_add_fusion.1
  1089.9 4.8 reduce-scatter.40.cloned.1.call-done
  1096.4 22.6 %reduce-scatter.38.cloned.1.call-done = bf16[288,144]{1,0:T(8,128)(2,1)} async-done(((bf16[1152,144]{1,0:T(8,128)(2,1)}), bf16[288,144]{1,0:T(8,128)(2,1)}) %reduce-scatter.38.cloned.1.call-update) | async-done | bytes 82960
  1120.8 22.8 %reduce-scatter.36.cloned.1.call-done = bf16[288,144]{1,0:T(8,128)(2,1)} async-done(((bf16[1152,144]{1,0:T(8,128)(2,1)}), bf16[288,144]{1,0:T(8,128)(2,1)}) %reduce-scatter.36.cloned.1.call-update) | async-done | bytes 82960
  1145.4 23.2 %reduce-scatter.34.cloned.1.call-done = bf16[288,144]{1,0:T(8,128)(2,1)} async-done(((bf16[1152,144]{1,0:T(8,128)(2,1)}), bf16[288,144]{1,0:T(8,128)(2,1)}) %reduce-scatter.34.cloned.1.call-update) | async-done | bytes 82960
  1170.3 97.1 %reduce-scatter.28.cloned.1.call-done = bf16[256,1152]{1,0:T(8,128)(2,1)} async-done(((bf16[2048,1152]{1,0:T(8,128)(2,1)}), bf16[256,1152]{1,0:T(8,128)(2,1)}) %reduce-scatter.28.cloned.1.call-update) | async-done | bytes 589840 | tf_op jit(solution)/shard_map/reduce_scatter | solution.py:337
  1269.4 36.3 %all-reduce.17 = (f32[1152]{0:T(1024)S(1)}, f32[1152]{0:T(1024)S(1)}, f32[1152]{0:T(1024)S(1)}, f32[1152]{0:T(1024)S(1)}, f32[1152]{0:T(1024)S(1)}, /*index=5*/f32[1152]{0:T(1024)S(1)}) all-reduce(f32[1152]{0:T(1024)S(1)} %get-tuple-element.226, f32[1152]{0:T(1024)S(1)} %get-tuple-element.231, ...), channel_id=7, replica_groups=mesh['gx'=4,'gy'=8] {'gy'}, use_global_device_ids=true, to_apply=%region_29.30.clone | all-reduce | flops 6912 | bytes 55296
  1306.2 10.7 all-reduce.18
  (382 shorter events, 241.3 us)
Async XLA Ops:
  8.1 86.1 %all-gather.17.cloned.1.call-start = ((), (), s32[]{:S(2)}) async-start(), calls=%async_computation.11 | async-start | bytes 5308416 | tf_op jit(solution)/shard_map/all_gather | solution.py:133
  8.8 223.0 %reduce-scatter.20.cloned.1.call-start = ((), (), s32[]{:S(2)}) async-start(), calls=%async_computation.12 | async-start | bytes 5308416 | tf_op jit(solution)/shard_map/reduce_scatter | solution.py:147
  138.2 131.3 %copy-start.40 = (bf16[538]{0:T(1024)(128)(2,1)S(1)}, bf16[538]{0:T(1024)(128)(2,1)}, u32[]{:S(2)}) copy-start(bf16[538]{0:T(1024)(128)(2,1)} %param.36) | copy-start | bytes 3232
  138.2 200.3 %all-gather.19.cloned.1.call-start = ((), (), s32[]{:S(2)}) async-start(), calls=%async_computation.13 | async-start | bytes 1843200 | tf_op jit(solution)/shard_map/all_gather | solution.py:129
  138.8 199.8 %all-gather.21.cloned.1.call-start = ((), (), s32[]{:S(2)}) async-start(), calls=%async_computation.14 | async-start | bytes 1843200 | tf_op jit(solution)/shard_map/all_gather | solution.py:130
  235.3 26.7 %collective-permute-start = (bf16[256,1152]{1,0:T(8,128)(2,1)S(1)}, bf16[256,1152]{1,0:T(8,128)(2,1)S(1)}, u32[]{:S(2)}, u32[]{:S(2)}) collective-permute-start(bf16[256,1152]{1,0:T(8,128)(2,1)S(1)} %get-tuple-element.303), channel_id=1, source_target_pairs={{0,1},{1,2},{2,3},{3,4},{4,5},{5,6},{6,7},{7,0},{8,9},{9,10},{10,1... | collective-permute-start | bytes 1769480 | tf_op jit(solution)/shard_map/ppermute | solution.py:166
  236.8 27.7 %collective-permute-start.1 = (bf16[256,1152]{1,0:T(8,128)(2,1)S(1)}, bf16[256,1152]{1,0:T(8,128)(2,1)S(1)}, u32[]{:S(2)}, u32[]{:S(2)}) collective-permute-start(bf16[256,1152]{1,0:T(8,128)(2,1)S(1)} %get-tuple-element.303), channel_id=1, source_target_pairs={{0,7},{1,0},{2,1},{3,2},{4,3},{5,4},{6,5},{7,6},{8,15},{9,8},{10,9... | collective-permute-start | bytes 1769480 | tf_op jit(solution)/shard_map/ppermute | solution.py:171
  262.0 26.8 %collective-permute-start.2 = (bf16[256,1152]{1,0:T(8,128)(2,1)S(1)}, bf16[256,1152]{1,0:T(8,128)(2,1)S(1)}, u32[]{:S(2)}, u32[]{:S(2)}) collective-permute-start(bf16[256,1152]{1,0:T(8,128)(2,1)S(1)} %collective-permute-done), channel_id=1, source_target_pairs={{0,1},{1,2},{2,3},{3,4},{4,5},{5,6},{6,7},{7,0},{8,9},{9,10},{10,1... | collective-permute-start | bytes 1769480 | tf_op jit(solution)/shard_map/ppermute | solution.py:166
  264.5 28.6 %collective-permute-start.3 = (bf16[256,1152]{1,0:T(8,128)(2,1)S(1)}, bf16[256,1152]{1,0:T(8,128)(2,1)S(1)}, u32[]{:S(2)}, u32[]{:S(2)}) collective-permute-start(bf16[256,1152]{1,0:T(8,128)(2,1)S(1)} %collective-permute-done.1), channel_id=1, source_target_pairs={{0,7},{1,0},{2,1},{3,2},{4,3},{5,4},{6,5},{7,6},{8,15},{9,8},{10,9... | collective-permute-start | bytes 1769480 | tf_op jit(solution)/shard_map/ppermute | solution.py:171
  266.7 180.1 %reduce-scatter.22.cloned.1.call-start = ((), (), s32[]{:S(2)}) async-start(), calls=%async_computation.15 | async-start | bytes 5308416 | tf_op jit(solution)/shard_map/reduce_scatter | solution.py:190
  288.8 26.1 %collective-permute-start.4 = (bf16[256,1152]{1,0:T(8,128)(2,1)S(1)}, bf16[256,1152]{1,0:T(8,128)(2,1)S(1)}, u32[]{:S(2)}, u32[]{:S(2)}) collective-permute-start(bf16[256,1152]{1,0:T(8,128)(2,1)S(1)} %collective-permute-done.2), channel_id=1, source_target_pairs={{0,1},{1,2},{2,3},{3,4},{4,5},{5,6},{6,7},{7,0},{8,9},{9,10},{10,1... | collective-permute-start | bytes 1769480 | tf_op jit(solution)/shard_map/ppermute | solution.py:166
  293.0 26.5 %collective-permute-start.5 = (bf16[256,1152]{1,0:T(8,128)(2,1)S(1)}, bf16[256,1152]{1,0:T(8,128)(2,1)S(1)}, u32[]{:S(2)}, u32[]{:S(2)}) collective-permute-start(bf16[256,1152]{1,0:T(8,128)(2,1)S(1)} %collective-permute-done.3), channel_id=1, source_target_pairs={{0,7},{1,0},{2,1},{3,2},{4,3},{5,4},{6,5},{7,6},{8,15},{9,8},{10,9... | collective-permute-start | bytes 1769480 | tf_op jit(solution)/shard_map/ppermute | solution.py:171
  314.9 15.9 %collective-permute-start.6 = (bf16[256,1152]{1,0:T(8,128)(2,1)S(1)}, bf16[256,1152]{1,0:T(8,128)(2,1)S(1)}, u32[]{:S(2)}, u32[]{:S(2)}) collective-permute-start(bf16[256,1152]{1,0:T(8,128)(2,1)S(1)} %collective-permute-done.4), channel_id=1, source_target_pairs={{0,1},{1,2},{2,3},{3,4},{4,5},{5,6},{6,7},{7,0},{8,9},{9,10},{10,1... | collective-permute-start | bytes 1769480 | tf_op jit(solution)/shard_map/ppermute | solution.py:166
  351.6 98.6 %copy-start.53 = (bf16[144]{0:T(256)(128)(2,1)S(1)}, bf16[144]{0:T(256)(128)(2,1)}, u32[]{:S(2)}) copy-start(bf16[144]{0:T(256)(128)(2,1)} %param.34) | copy-start | bytes 868
  351.6 136.0 %copy-start.22 = (bf16[288,144]{0,1:T(8,128)(2,1)S(1)}, bf16[288,144]{0,1:T(8,128)(2,1)}, u32[]{:S(2)}) copy-start(bf16[288,144]{0,1:T(8,128)(2,1)} %param.28) | copy-start | bytes 248836
  351.6 143.0 %copy-start.23 = (bf16[288,144]{0,1:T(8,128)(2,1)S(1)}, bf16[288,144]{0,1:T(8,128)(2,1)}, u32[]{:S(2)}) copy-start(bf16[288,144]{0,1:T(8,128)(2,1)} %param.26) | copy-start | bytes 248836
  351.6 150.3 %copy-start.55 = (bf16[144]{0:T(256)(128)(2,1)S(1)}, bf16[144]{0:T(256)(128)(2,1)}, u32[]{:S(2)}) copy-start(bf16[144]{0:T(256)(128)(2,1)} %param.27) | copy-start | bytes 868
  351.6 150.3 %copy-start.24 = (bf16[288,144]{0,1:T(8,128)(2,1)S(1)}, bf16[288,144]{0,1:T(8,128)(2,1)}, u32[]{:S(2)}) copy-start(bf16[288,144]{0,1:T(8,128)(2,1)} %param.29) | copy-start | bytes 248836
  351.7 177.7 %all-gather.23.cloned.1.call-start = ((), (), s32[]{:S(2)}) async-start(), calls=%async_computation.16 | async-start | bytes 5308416 | tf_op jit(solution)/shard_map/all_gather | solution.py:133
  351.7 157.6 %copy-start.56 = (bf16[144]{0:T(256)(128)(2,1)S(1)}, bf16[144]{0:T(256)(128)(2,1)}, u32[]{:S(2)}) copy-start(bf16[144]{0:T(256)(128)(2,1)} %param.30) | copy-start | bytes 868
  351.7 157.6 %copy-start.26 = (bf16[144,288]{1,0:T(8,128)(2,1)S(1)}, bf16[144,288]{1,0:T(8,128)(2,1)}, u32[]{:S(2)}) copy-start(bf16[144,288]{1,0:T(8,128)(2,1)} %param.31) | copy-start | bytes 248836
  449.0 249.5 %reduce-scatter.24.cloned.1.call-start = ((), (), s32[]{:S(2)}) async-start(), calls=%async_computation.17 | async-start | bytes 5308416 | tf_op jit(solution)/shard_map/reduce_scatter | solution.py:147
  567.8 133.3 %copy-start.4 = (bf16[256,1152]{1,0:T(8,128)(2,1)S(1)}, bf16[256,1152]{1,0:T(8,128)(2,1)}, u32[]{:S(2)}) copy-start(bf16[256,1152]{1,0:T(8,128)(2,1)} %param.23) | copy-start | bytes 1769476
  567.9 237.1 %all-gather.29.cloned.1.call-start = ((), (), s32[]{:S(2)}) async-start(), calls=%async_computation.20 | async-start | bytes 1843200 | tf_op jit(solution)/shard_map/all_gather | solution.py:129
  568.5 245.0 %all-gather.27.cloned.1.call-start = ((), (), s32[]{:S(2)}) async-start(), calls=%async_computation.19 | async-start | bytes 5308416 | tf_op jit(solution)/shard_map/all_gather | solution.py:287
  569.2 244.2 %all-gather.25.cloned.1.call-start = ((), (), s32[]{:S(2)}) async-start(), calls=%async_computation.18 | async-start | bytes 1843200 | tf_op jit(solution)/shard_map/all_gather | solution.py:130
  702.1 26.4 %collective-permute-start.7 = (bf16[256,1152]{1,0:T(8,128)(2,1)S(1)}, bf16[256,1152]{1,0:T(8,128)(2,1)S(1)}, u32[]{:S(2)}, u32[]{:S(2)}) collective-permute-start(bf16[256,1152]{1,0:T(8,128)(2,1)S(1)} %get-tuple-element.301), channel_id=1, source_target_pairs={{0,1},{1,2},{2,3},{3,4},{4,5},{5,6},{6,7},{7,0},{8,9},{9,10},{10,1... | collective-permute-start | bytes 1769480 | tf_op jit(solution)/shard_map/ppermute | solution.py:166
  703.5 27.4 %collective-permute-start.8 = (bf16[256,1152]{1,0:T(8,128)(2,1)S(1)}, bf16[256,1152]{1,0:T(8,128)(2,1)}, u32[]{:S(2)}, u32[]{:S(2)}) collective-permute-start(bf16[256,1152]{1,0:T(8,128)(2,1)S(1)} %get-tuple-element.301), channel_id=1, source_target_pairs={{0,7},{1,0},{2,1},{3,2},{4,3},{5,4},{6,5},{7,6},{8,15},{9,8},{10,9... | collective-permute-start | bytes 1769480 | tf_op jit(solution)/shard_map/ppermute | solution.py:171
  728.5 26.5 %collective-permute-start.9 = (bf16[256,1152]{1,0:T(8,128)(2,1)S(1)}, bf16[256,1152]{1,0:T(8,128)(2,1)S(1)}, u32[]{:S(2)}, u32[]{:S(2)}) collective-permute-start(bf16[256,1152]{1,0:T(8,128)(2,1)S(1)} %collective-permute-done.7), channel_id=1, source_target_pairs={{0,1},{1,2},{2,3},{3,4},{4,5},{5,6},{6,7},{7,0},{8,9},{9,10},{10,1... | collective-permute-start | bytes 1769480 | tf_op jit(solution)/shard_map/ppermute | solution.py:166
  731.0 29.3 %collective-permute-start.10 = (bf16[256,1152]{1,0:T(8,128)(2,1)}, bf16[256,1152]{1,0:T(8,128)(2,1)S(1)}, u32[]{:S(2)}, u32[]{:S(2)}) collective-permute-start(bf16[256,1152]{1,0:T(8,128)(2,1)} %collective-permute-done.8), channel_id=1, source_target_pairs={{0,7},{1,0},{2,1},{3,2},{4,3},{5,4},{6,5},{7,6},{8,15},{9,8},{10,9... | collective-permute-start | bytes 1769480 | tf_op jit(solution)/shard_map/ppermute | solution.py:171
  737.1 189.6 %reduce-scatter.26.cloned.1.call-start = ((), (), s32[]{:S(2)}) async-start(), calls=%async_computation.21 | async-start | bytes 5308416 | tf_op jit(solution)/shard_map/reduce_scatter | solution.py:305
  755.0 26.1 %collective-permute-start.11 = (bf16[256,1152]{1,0:T(8,128)(2,1)S(1)}, bf16[256,1152]{1,0:T(8,128)(2,1)S(1)}, u32[]{:S(2)}, u32[]{:S(2)}) collective-permute-start(bf16[256,1152]{1,0:T(8,128)(2,1)S(1)} %collective-permute-done.9), channel_id=1, source_target_pairs={{0,1},{1,2},{2,3},{3,4},{4,5},{5,6},{6,7},{7,0},{8,9},{9,10},{10,1... | collective-permute-start | bytes 1769480 | tf_op jit(solution)/shard_map/ppermute | solution.py:166
  760.3 25.1 %collective-permute-start.12 = (bf16[256,1152]{1,0:T(8,128)(2,1)S(1)}, bf16[256,1152]{1,0:T(8,128)(2,1)S(1)}, u32[]{:S(2)}, u32[]{:S(2)}) collective-permute-start(bf16[256,1152]{1,0:T(8,128)(2,1)S(1)} %collective-permute-done.10), channel_id=1, source_target_pairs={{0,7},{1,0},{2,1},{3,2},{4,3},{5,4},{6,5},{7,6},{8,15},{9,8},{10,9... | collective-permute-start | bytes 1769480 | tf_op jit(solution)/shard_map/ppermute | solution.py:171
  781.1 16.1 %collective-permute-start.13 = (bf16[256,1152]{1,0:T(8,128)(2,1)S(1)}, bf16[256,1152]{1,0:T(8,128)(2,1)S(1)}, u32[]{:S(2)}, u32[]{:S(2)}) collective-permute-start(bf16[256,1152]{1,0:T(8,128)(2,1)S(1)} %collective-permute-done.11), channel_id=1, source_target_pairs={{0,1},{1,2},{2,3},{3,4},{4,5},{5,6},{6,7},{7,0},{8,9},{9,10},{10,1... | collective-permute-start | bytes 1769480 | tf_op jit(solution)/shard_map/ppermute | solution.py:166
  832.8 178.9 %all-gather.31.cloned.1.call-start = ((), (), s32[]{:S(2)}) async-start(), calls=%async_computation.22 | async-start | bytes 5308416 | tf_op jit(solution)/shard_map/all_gather | solution.py:319
  932.6 151.9 %reduce-scatter.32.cloned.1.call-start = ((), (), s32[]{:S(2)}) async-start(), calls=%async_computation.25 | async-start | bytes 1843200 | tf_op jit(solution)/shard_map/reduce_scatter | solution.py:298
  941.8 144.6 %reduce-scatter.30.cloned.1.call-start = ((), (), s32[]{:S(2)}) async-start(), calls=%async_computation.24 | async-start | bytes 1843200 | tf_op jit(solution)/shard_map/reduce_scatter | solution.py:292
  950.7 144.0 %reduce-scatter.40.cloned.1.call-start = ((), (), s32[]{:S(2)}) async-start(), calls=%async_computation.29 | async-start | bytes 737280
  1022.9 96.1 %reduce-scatter.38.cloned.1.call-start = ((), (), s32[]{:S(2)}) async-start(), calls=%async_computation.28 | async-start | bytes 737280
  1055.1 88.6 %reduce-scatter.36.cloned.1.call-start = ((), (), s32[]{:S(2)}) async-start(), calls=%async_computation.27 | async-start | bytes 737280
  1061.1 107.5 %reduce-scatter.34.cloned.1.call-start = ((), (), s32[]{:S(2)}) async-start(), calls=%async_computation.26 | async-start | bytes 737280
  1073.6 193.8 %reduce-scatter.28.cloned.1.call-start = ((), (), s32[]{:S(2)}) async-start(), calls=%async_computation.23 | async-start | bytes 5308416 | tf_op jit(solution)/shard_map/reduce_scatter | solution.py:337
  1083.0 184.5 %copy-start.28 = (f32[1152]{0:T(1024)S(1)}, f32[1152]{0:T(1024)}, u32[]{:S(2)}) copy-start(f32[1152]{0:T(1024)} %copy-done.27) | copy-start | bytes 13828
  1083.0 186.3 %copy-start.36 = (f32[1152]{0:T(1024)S(1)}, f32[1152]{0:T(1024)}, u32[]{:S(2)}) copy-start(f32[1152]{0:T(1024)} %get-tuple-element.224) | copy-start | bytes 13828
  1083.0 186.3 %copy-start.37 = (f32[1152]{0:T(1024)S(1)}, f32[1152]{0:T(1024)}, u32[]{:S(2)}) copy-start(f32[1152]{0:T(1024)} %get-tuple-element.230) | copy-start | bytes 13828
  1083.0 186.3 %copy-start.38 = (f32[1152]{0:T(1024)S(1)}, f32[1152]{0:T(1024)}, u32[]{:S(2)}) copy-start(f32[1152]{0:T(1024)} %get-tuple-element.298) | copy-start | bytes 13828
  1083.0 186.3 %copy-start.39 = (f32[1152]{0:T(1024)S(1)}, f32[1152]{0:T(1024)}, u32[]{:S(2)}) copy-start(f32[1152]{0:T(1024)} %get-tuple-element.312) | copy-start | bytes 13828
  1083.1 223.1 %copy-start.45 = (f32[538]{0:T(1024)S(1)}, f32[538]{0:T(1024)}, u32[]{:S(2)}) copy-start(f32[538]{0:T(1024)} %get-tuple-element.315) | copy-start | bytes 6460
  (47 other events, 1165.0 us)
Sparse Core Ops, SparseCore 0:
  11.1 83.0 all-gather.16
  138.3 93.3 reduce-scatter.19
  351.7 95.0 reduce-scatter.21
  449.1 80.1 all-gather.22
  568.0 130.4 reduce-scatter.23
Sparse Core Ops, SparseCore 1:
  140.2 17.1 all-gather.18
  266.8 17.2 all-gather.20
  569.9 17.1 all-gather.28
  589.3 101.6 all-gather.26
  737.1 17.4 all-gather.24
  832.9 93.6 reduce-scatter.25
  932.6 79.1 all-gather.30
  1014.2 25.8 reduce-scatter.31
  1042.6 27.4 reduce-scatter.29
  1072.7 22.0 reduce-scatter.39
  1097.1 22.0 reduce-scatter.37
  1121.6 22.0 reduce-scatter.35
  1146.6 22.0 reduce-scatter.33
  1172.2 95.2 reduce-scatter.27
